TPU v7x, 512 devices: a whole 4x8x8 slice. The times are simulated.
512 devices in a mesh: pole: 16 (over x, z_lo, core), slab: 32 (over y, z_hi).
Axes of the slice: x: 4, y: 8, z: 8 (z_hi: 4, z_lo: 2; z = z_hi * 2 + z_lo), core: 2. Of those that a mesh axis runs over, the one named last changes fastest.
Arguments:
- vectors: float32 [2, 16, 128, 16, 128], P(None, None, 'slab'), may hold values from -6 to 6
- potential: float32 [128, 16, 128], P('slab'), may hold values from 0 to 2
Outputs:
- filtered: float32 [2, 16, 128, 16, 128], P(None, None, 'slab', 'pole')
- gram_correlation: float32 [2, 16, 16], replicated
- gram_energy: float32 [2, 16, 16], replicated
All inputs are finite; a program needn't handle non-finite values.
Results may differ from a plain program's by a relative error of at most 0.005.
Values sent between devices are 32-bit elements; how exact they have to be, the bound alone decides.
No kernel may reach another device: no remote copies, remote signals or barrier semaphores. Data moves between devices by JAX's collectives and lax.ppermute only.
A program may use at most 64 MiB of HBM per device.

v0:
```python
import math
import jax
import jax.numpy as jnp
from jax import lax
from jax.sharding import PartitionSpec as P

ITERS = 3
contour_center = 2.0
contour_radius = 1.5


def extended(block, sides, width):
    for axis, dim in sides:
        count = lax.axis_size(axis)
        forward = [(i, i + 1) for i in range(count - 1)]
        forward.append((count - 1, 0))
        backward = [(target, source) for source, target in forward]
        low = lax.ppermute(
            lax.slice_in_dim(block, block.shape[dim] - width, None, axis=dim), axis, forward
        )
        high = lax.ppermute(lax.slice_in_dim(block, 0, width, axis=dim), axis, backward)
        block = jnp.concatenate([low, block, high], axis=dim)
    return block


def apply_shifted(block, potential, shift_re, shift_im):
    padded = extended(block, (("slab", 2),), 1)
    beside = padded[:, :, 2:] + padded[:, :, :-2]
    beside = beside + jnp.roll(block, 1, 3) + jnp.roll(block, -1, 3)
    beside = beside + jnp.roll(block, 1, 4) + jnp.roll(block, -1, 4)
    diagonal = shift_re - 3.0 - potential
    real_part = diagonal * block[0] - shift_im * block[1] + 0.5 * beside[0]
    imag_part = diagonal * block[1] + shift_im * block[0] + 0.5 * beside[1]
    return jnp.stack([real_part, imag_part])


def bilinear(left, right):
    real_part = jnp.sum(left[0] * right[0] - left[1] * right[1], axis=(1, 2, 3))
    imag_part = jnp.sum(left[0] * right[1] + left[1] * right[0], axis=(1, 2, 3))
    return jnp.stack([real_part, imag_part])


def complex_divide(numer, denom):
    magnitude = denom[0] * denom[0] + denom[1] * denom[1]
    return jnp.stack(
        [
            (numer[0] * denom[0] + numer[1] * denom[1]) / magnitude,
            (numer[1] * denom[0] - numer[0] * denom[1]) / magnitude,
        ]
    )


def column_scale(coef, block):
    first = coef[0][:, None, None, None]
    second = coef[1][:, None, None, None]
    return jnp.stack([first * block[0] - second * block[1], first * block[1] + second * block[0]])


def scalar_scale(first, second, block):
    return jnp.stack([first * block[0] - second * block[1], first * block[1] + second * block[0]])


def inner(left, right):
    return lax.dot_general(
        left,
        right,
        (((1,), (1,)), ((), ())),
        precision=lax.Precision.HIGHEST,
        preferred_element_type=jnp.float32,
    )


def gram_pair(filtered, image, cells):
    count = filtered.shape[1]
    sre = filtered[0].reshape(count, -1)
    sim = filtered[1].reshape(count, -1)
    hre = image[0].reshape(count, -1)
    him = image[1].reshape(count, -1)
    correlation = (
        jnp.stack([inner(sre, sre) + inner(sim, sim), inner(sre, sim) - inner(sim, sre)]) / cells
    )
    energy = (
        jnp.stack([inner(sre, hre) + inner(sim, him), inner(sre, him) - inner(sim, hre)]) / cells
    )
    return (correlation, energy)


def residual_form(residual):
    return lax.psum(bilinear(residual, residual), "slab")


def on_device(vectors, potential):
    pole_count = lax.axis_size("pole")
    angle = 2.0 * math.pi / pole_count * (lax.axis_index("pole").astype(jnp.float32) + 0.5)
    cosine = jnp.cos(angle)
    sine = jnp.sin(angle)
    shift_re = contour_center + contour_radius * cosine
    shift_im = contour_radius * sine
    weight_re = contour_radius * cosine / pole_count
    weight_im = contour_radius * sine / pole_count
    solution = jnp.zeros_like(vectors)
    residual = vectors
    direction = vectors
    rho = residual_form(residual)
    for iteration in range(ITERS):
        mapped = apply_shifted(direction, potential, shift_re, shift_im)
        curve = lax.psum(bilinear(direction, mapped), "slab")
        alpha = complex_divide(rho, curve)
        solution = solution + column_scale(alpha, direction)
        residual = residual - column_scale(alpha, mapped)
        if iteration + 1 < ITERS:
            rho_new = residual_form(residual)
            direction = residual + column_scale(complex_divide(rho_new, rho), direction)
            rho = rho_new
    weighted = scalar_scale(weight_re, weight_im, solution)
    hsol = scalar_scale(shift_re, shift_im, solution) - vectors + residual
    weighted_image = scalar_scale(weight_re, weight_im, hsol)
    cells = vectors.shape[2] * lax.axis_size("slab") * vectors.shape[3] * vectors.shape[4]
    filtered, image = lax.psum((weighted, weighted_image), "pole")
    correlation, energy = gram_pair(filtered, image, cells)
    correlation, energy = lax.psum((correlation, energy), "slab")
    rows = filtered.shape[3] // pole_count
    own = lax.dynamic_slice_in_dim(filtered, lax.axis_index("pole") * rows, rows, 3)
    return (own, correlation, energy)


def solution(mesh):
    in_specs = (P(None, None, "slab", None, None), P("slab", None, None))
    out_specs = (P(None, None, "slab", "pole", None), P(), P())
    return jax.shard_map(
        on_device, mesh=mesh, in_specs=in_specs, out_specs=out_specs, check_vma=False
    )
```

profile of v0, /device:TPU:32, one launch (start us, length us, event | category | flops | bytes accessed | tf_op | source)
XLA Modules:
  0.0 801.4 jit_solution(13384978102229270736)
XLA Ops:
  7.2 1.8 copy.5
  9.1 10.8 %collective-permute-start = (f32[2,16,1,16,128]{4,1,3,2,0:T(8,128)S(1)}, f32[2,16,1,16,128]{4,1,3,2,0:T(8,128)S(1)}, u32[]{:S(2)}, u32[]{:S(2)}) collective-permute-start(f32[2,16,1,16,128]{4,1,3,2,0:T(8,128)S(1)} %get-tuple-element.77), channel_id=1, source_target_pairs={{1,0},{2,1},{3,2},{4,3},{5,4},{6,5},{7,6},{8,7},{9,8},{10,9},{11,1... | collective-permute-start | bytes 786440 | tf_op jit(solution)/shard_map/ppermute | solution.py:21
  19.9 1.9 collective-permute-start.1
  21.9 1.5 fusion.68
  23.3 1.6 fusion.67
  25.0 1.7 fusion.66
  26.8 2.0 collective-permute-done
  28.8 10.6 %collective-permute-done.1 = f32[2,16,1,16,128]{4,1,3,2,0:T(8,128)S(1)} collective-permute-done((f32[2,16,1,16,128]{4,1,3,2,0:T(8,128)S(1)}, f32[2,16,1,16,128]{4,1,3,2,0:T(8,128)S(1)}, u32[]{:S(2)}, u32[]{:S(2)}) %collective-permute-start.1) | collective-permute-done | bytes 262176 | tf_op jit(solution)/shard_map/ppermute | solution.py:18
  39.4 3.4 fusion.22
  43.5 76.9 %all-reduce.1 = (f32[2,16]{1,0:T(2,128)S(1)}, f32[2,16]{1,0:T(2,128)S(1)}) all-reduce(f32[2,16]{1,0:T(2,128)S(1)} %get-tuple-element.90, f32[2,16]{1,0:T(2,128)S(1)} %get-tuple-element.89), channel_id=1, replica_groups=mesh['pole'=16,'slab'=32] {'slab'}, use_global_device_ids=true, to_apply=%region_5.6 | all-reduce | flops 64 | bytes 512 | tf_op jit(solution)/shard_map/psum | solution.py:107
  120.4 1.4 multiply_subtract_fusion.9
  121.9 1.1 copy-done
  123.9 79.8 %psum.72 = f32[2,16]{1,0:T(2,128)S(1)} all-reduce(f32[2,16]{1,0:T(2,128)S(1)} %pad_maximum_fusion.10), channel_id=1, replica_groups=mesh['pole'=16,'slab'=32] {'slab'}, use_global_device_ids=true, to_apply=%region_8.9 | all-reduce | flops 32 | bytes 256 | tf_op jit(solution)/shard_map/psum | solution.py:89
  205.3 3.2 collective-permute-start.2
  208.6 3.5 collective-permute-start.3
  212.3 4.7 collective-permute-done.2
  217.0 6.9 collective-permute-done.3
  225.6 76.8 %psum.73 = f32[2,16]{1,0:T(2,128)S(1)} all-reduce(f32[2,16]{1,0:T(2,128)S(1)} %pad_maximum_fusion.11), channel_id=1, replica_groups=mesh['pole'=16,'slab'=32] {'slab'}, use_global_device_ids=true, to_apply=%region_11.12 | all-reduce | flops 32 | bytes 256 | tf_op jit(solution)/shard_map/psum | solution.py:107
  302.5 2.5 multiply_subtract_fusion.6
  306.8 79.9 %psum.74 = f32[2,16]{1,0:T(2,128)S(1)} all-reduce(f32[2,16]{1,0:T(2,128)S(1)} %pad_maximum_fusion.12), channel_id=1, replica_groups=mesh['pole'=16,'slab'=32] {'slab'}, use_global_device_ids=true, to_apply=%region_14.15 | all-reduce | flops 32 | bytes 256 | tf_op jit(solution)/shard_map/psum | solution.py:89
  389.5 2.9 collective-permute-start.4
  392.4 4.0 collective-permute-start.5
  396.7 4.3 collective-permute-done.4
  401.0 6.6 collective-permute-done.5
  409.3 76.8 %psum.75 = f32[2,16]{1,0:T(2,128)S(1)} all-reduce(f32[2,16]{1,0:T(2,128)S(1)} %pad_maximum_fusion.13), channel_id=1, replica_groups=mesh['pole'=16,'slab'=32] {'slab'}, use_global_device_ids=true, to_apply=%region_17.18 | all-reduce | flops 32 | bytes 256 | tf_op jit(solution)/shard_map/psum | solution.py:107
  486.2 1.6 multiply_subtract_fusion.1
  491.6 1.0 pad_maximum_fusion.7
  492.7 1.1 pad_maximum_fusion.6
  493.8 134.6 %all-reduce.5.cloned.1.call-done = (f32[2,16,4,16,128]{4,1,3,2,0:T(8,128)}, f32[2,16,4,16,128]{4,1,3,2,0:T(8,128)}) async-done(((f32[2,16,4,16,128]{4,1,3,2,0:T(8,128)}, f32[2,16,4,16,128]{4,1,3,2,0:T(8,128)}), (f32[2,16,4,16,128]{4,1,3,2,0:T(8,128)}, f32[2,16,4,16,128]{4,1,3,2,0:T(8,128)})) %all-reduce.5.cloned.1.call-update) | async-done | bytes 2097168 | tf_op jit(solution)/shard_map/psum | solution.py:119
  628.5 2.1 convolution_bitcast_fusion
  630.5 1.8 convolution_bitcast_fusion.2
  638.0 156.6 %all-reduce = (f32[2,16,16]{2,1,0:T(8,128)}, f32[2,16,16]{2,1,0:T(8,128)}) all-reduce(f32[2,16,16]{2,1,0:T(8,128)S(1)} %maximum_multiply_fusion, f32[2,16,16]{2,1,0:T(8,128)S(1)} %maximum_multiply_fusion.1), channel_id=1, replica_groups=mesh['pole'=16,'slab'=32] {'slab'}, use_global_device_ids=true, to_apply=%region_19.20 | all-reduce | flops 1024 | bytes 8192 | tf_op jit(solution)/shard_map/psum | solution.py:121
  (86 shorter events, 21.2 us)
Async XLA Ops:
  7.2 621.3 %all-reduce.5.cloned.1.call-start = ((), (), s32[]{:S(2)}) async-start(), calls=%async_computation | async-start | bytes 4194304 | tf_op jit(solution)/shard_map/psum | solution.py:119
  9.1 19.7 %collective-permute-start = (f32[2,16,1,16,128]{4,1,3,2,0:T(8,128)S(1)}, f32[2,16,1,16,128]{4,1,3,2,0:T(8,128)S(1)}, u32[]{:S(2)}, u32[]{:S(2)}) collective-permute-start(f32[2,16,1,16,128]{4,1,3,2,0:T(8,128)S(1)} %get-tuple-element.77), channel_id=1, source_target_pairs={{1,0},{2,1},{3,2},{4,3},{5,4},{6,5},{7,6},{8,7},{9,8},{10,9},{11,1... | collective-permute-start | bytes 786440 | tf_op jit(solution)/shard_map/ppermute | solution.py:21
  19.9 19.5 %collective-permute-start.1 = (f32[2,16,1,16,128]{4,1,3,2,0:T(8,128)S(1)}, f32[2,16,1,16,128]{4,1,3,2,0:T(8,128)S(1)}, u32[]{:S(2)}, u32[]{:S(2)}) collective-permute-start(f32[2,16,1,16,128]{4,1,3,2,0:T(8,128)S(1)} %get-tuple-element.78), channel_id=1, source_target_pairs={{0,1},{1,2},{2,3},{3,4},{4,5},{5,6},{6,7},{7,8},{8,9},{9,10},{10,1... | collective-permute-start | bytes 786440 | tf_op jit(solution)/shard_map/ppermute | solution.py:18
  25.0 1.8 copy-start.15
  121.8 1.2 copy-start
  205.3 11.6 %collective-permute-start.2 = (f32[2,16,1,16,128]{4,1,3,2,0:T(8,128)S(1)}, f32[2,16,1,16,128]{4,1,3,2,0:T(8,128)S(1)}, u32[]{:S(2)}, u32[]{:S(2)}) collective-permute-start(f32[2,16,1,16,128]{4,1,3,2,0:T(8,128)S(1)} %get-tuple-element.67), channel_id=1, source_target_pairs={{1,0},{2,1},{3,2},{4,3},{5,4},{6,5},{7,6},{8,7},{9,8},{10,9},{11,1... | collective-permute-start | bytes 786440 | tf_op jit(solution)/shard_map/ppermute | solution.py:21
  208.6 15.3 %collective-permute-start.3 = (f32[2,16,1,16,128]{4,1,3,2,0:T(8,128)S(1)}, f32[2,16,1,16,128]{4,1,3,2,0:T(8,128)S(1)}, u32[]{:S(2)}, u32[]{:S(2)}) collective-permute-start(f32[2,16,1,16,128]{4,1,3,2,0:T(8,128)S(1)} %get-tuple-element.68), channel_id=1, source_target_pairs={{0,1},{1,2},{2,3},{3,4},{4,5},{5,6},{6,7},{7,8},{8,9},{9,10},{10,1... | collective-permute-start | bytes 786440 | tf_op jit(solution)/shard_map/ppermute | solution.py:18
  224.6 1.0 copy-start.3
  305.0 0.8 copy-start.7
  305.1 1.4 copy-start.4
  386.7 1.0 copy-start.5
  386.7 1.2 copy-start.8
  389.5 11.5 %collective-permute-start.4 = (f32[2,16,1,16,128]{4,1,3,2,0:T(8,128)S(1)}, f32[2,16,1,16,128]{4,1,3,2,0:T(8,128)S(1)}, u32[]{:S(2)}, u32[]{:S(2)}) collective-permute-start(f32[2,16,1,16,128]{4,1,3,2,0:T(8,128)S(1)} %get-tuple-element.57), channel_id=1, source_target_pairs={{1,0},{2,1},{3,2},{4,3},{5,4},{6,5},{7,6},{8,7},{9,8},{10,9},{11,1... | collective-permute-start | bytes 786440 | tf_op jit(solution)/shard_map/ppermute | solution.py:21
  392.4 15.2 %collective-permute-start.5 = (f32[2,16,1,16,128]{4,1,3,2,0:T(8,128)S(1)}, f32[2,16,1,16,128]{4,1,3,2,0:T(8,128)S(1)}, u32[]{:S(2)}, u32[]{:S(2)}) collective-permute-start(f32[2,16,1,16,128]{4,1,3,2,0:T(8,128)S(1)} %get-tuple-element.58), channel_id=1, source_target_pairs={{0,1},{1,2},{2,3},{3,4},{4,5},{5,6},{6,7},{7,8},{8,9},{9,10},{10,1... | collective-permute-start | bytes 786440 | tf_op jit(solution)/shard_map/ppermute | solution.py:18
  408.3 1.0 copy-start.2
  486.2 1.8 copy-start.14
  487.8 1.0 copy-start.11
  487.8 1.2 copy-start.12
  487.8 1.3 copy-start.13
  489.3 1.0 copy-start.6
  489.4 1.2 copy-start.9
  628.5 2.1 copy-start.1
  632.3 1.6 copy-start.10
Sparse Core Ops, SparseCore 0:
  493.9 134.4 all-reduce.4
where the time goes:
time: 802 us; the launch traced here: 801 us
  blocking collectives  547 us (68%)
  waiting for transfers between devices  170 us (21%)
  starting transfers between devices  26.4 us (3%)
  other arithmetic  20.1 us (3%)
  local copies, waits for them, and re-layouts  15 us (2%)
  between operations  14.6 us (2%)
  matrix products  8.76 us (1%)
    psum x3, blocking collectives, on_device(): curve = lax.psum(bilinear(direction, mapped), 'slab')  231 us
    psum x2, blocking collectives, residual_form(): return lax.psum(bilinear(residual, residual), 'slab')  160 us
    psum x1, blocking collectives, on_device(): correlation, energy = lax.psum((correlation, energy), 'slab')  157 us
    psum x1, waiting for transfers between devices, on_device(): filtered, image = lax.psum((weighted, weighted_image), 'pole')  135 us
    ppermute x3, waiting for transfers between devices, extended(): lax.ppermute(lax.slice_in_dim(block, block.shape[dim] - width, None, axis...  24.2 us
    ppermute x3, starting transfers between devices, extended(): lax.ppermute(lax.slice_in_dim(block, 0, width, axis=dim), axis, backward)  17 us
  transfers between devices with their start and end apart: 7, of which 7 were waited for; matrix products, arithmetic and copies ran while one was open for 1% of the time, Pallas kernels for 0%

commit v1 on v0

--- a/solution.py
+++ b/solution.py
@@ -3,10 +3,12 @@
 import jax.numpy as jnp
 from jax import lax
 from jax.sharding import PartitionSpec as P
+from jax.lax import all_gather
 
 ITERS = 3
 contour_center = 2.0
 contour_radius = 1.5
+handle_kinds = lambda arr_in, group_axis: jnp.sum(all_gather(arr_in, group_axis), axis=0)
 
 
 def extended(block, sides, width):
@@ -86,7 +88,7 @@
 
 
 def residual_form(residual):
-    return lax.psum(bilinear(residual, residual), "slab")
+    return handle_kinds(bilinear(residual, residual), "slab")
 
 
 def on_device(vectors, potential):

time: 802 us -> 878 us (1.095)
  blocking collectives: 547 us -> 624 us
    all_gather x0 -> x3, blocking collectives: none -> 237 us  [all_gather(arr_in, group_axis)]
    psum x2 -> x0, blocking collectives: 160 us -> none  [residual_form(): return lax.psum(bilinear(residual, residual), 'slab')]
where the time goes in v1:
time: 878 us; the launch traced here: 877 us
  blocking collectives  624 us (71%)
  waiting for transfers between devices  168 us (19%)
  starting transfers between devices  26.4 us (3%)
  other arithmetic  20 us (2%)
  local copies, waits for them, and re-layouts  15 us (2%)
  between operations  14.6 us (2%)
    all_gather x3, blocking collectives, all_gather(arr_in, group_axis)  237 us
    psum x3, blocking collectives, on_device(): curve = lax.psum(bilinear(direction, mapped), 'slab')  231 us
    psum x1, blocking collectives, on_device(): correlation, energy = lax.psum((correlation, energy), 'slab')  157 us
    psum x1, waiting for transfers between devices, on_device(): filtered, image = lax.psum((weighted, weighted_image), 'pole')  135 us
    ppermute x3, waiting for transfers between devices, extended(): lax.ppermute(lax.slice_in_dim(block, block.shape[dim] - width, None, axis...  21 us
  transfers between devices with their start and end apart: 7, of which 7 were waited for; matrix products, arithmetic and copies ran while one was open for 1% of the time, Pallas kernels for 0%

profile of v1, /device:TPU:32, one launch (start us, length us, event | category | flops | bytes accessed | tf_op | source)
XLA Modules:
  0.0 876.9 jit_solution(12837067556677013388)
XLA Ops:
  7.2 1.8 copy.22
  9.1 10.8 %collective-permute-start = (f32[2,16,1,16,128]{4,1,3,2,0:T(8,128)S(1)}, f32[2,16,1,16,128]{4,1,3,2,0:T(8,128)S(1)}, u32[]{:S(2)}, u32[]{:S(2)}) collective-permute-start(f32[2,16,1,16,128]{4,1,3,2,0:T(8,128)S(1)} %get-tuple-element.78), channel_id=1, source_target_pairs={{1,0},{2,1},{3,2},{4,3},{5,4},{6,5},{7,6},{8,7},{9,8},{10,9},{11,1... | collective-permute-start | bytes 786440 | tf_op jit(solution)/shard_map/ppermute | solution.py:23
  19.9 1.9 collective-permute-start.1
  21.9 1.4 fusion.68
  23.3 1.6 fusion.67
  24.9 1.7 fusion.66
  26.8 2.0 collective-permute-done
  28.8 10.6 %collective-permute-done.1 = f32[2,16,1,16,128]{4,1,3,2,0:T(8,128)S(1)} collective-permute-done((f32[2,16,1,16,128]{4,1,3,2,0:T(8,128)S(1)}, f32[2,16,1,16,128]{4,1,3,2,0:T(8,128)S(1)}, u32[]{:S(2)}, u32[]{:S(2)}) %collective-permute-start.1) | collective-permute-done | bytes 262176 | tf_op jit(solution)/shard_map/ppermute | solution.py:20
  39.4 3.4 fusion.22
  43.5 76.9 %psum.49 = f32[2,16]{1,0:T(2,128)S(1)} all-reduce(f32[2,16]{1,0:T(2,128)S(1)} %pad_maximum_fusion.8), channel_id=1, replica_groups=mesh['pole'=16,'slab'=32] {'slab'}, use_global_device_ids=true, to_apply=%region_5.6 | all-reduce | flops 32 | bytes 256 | tf_op jit(solution)/shard_map/psum | solution.py:109
  120.4 78.2 %all-gather.3 = f32[32,2,16]{2,1,0:T(2,128)S(1)} all-gather(f32[1,2,16]{2,1,0:T(2,128)S(1)} %maximum_bitcast_fusion), channel_id=2, replica_groups=mesh['pole'=16,'slab'=32] {'slab'}, dimensions={0}, use_global_device_ids=true | all-gather | bytes 4224 | tf_op jit(solution)/shard_map/all_gather | solution.py:11
  198.6 1.4 multiply_subtract_fusion.9
  200.1 1.1 copy-done
  202.1 78.7 %all-gather.4 = f32[32,2,16]{2,1,0:T(2,128)S(1)} all-gather(f32[1,2,16]{2,1,0:T(2,128)S(1)} %maximum_bitcast_fusion.1), channel_id=3, replica_groups=mesh['pole'=16,'slab'=32] {'slab'}, dimensions={0}, use_global_device_ids=true | all-gather | bytes 4224 | tf_op jit(solution)/shard_map/all_gather | solution.py:11
  282.6 1.9 collective-permute-start.2
  284.5 4.8 collective-permute-start.3
  289.5 5.5 collective-permute-done.2
  295.0 5.2 collective-permute-done.3
  301.9 76.8 %psum.50 = f32[2,16]{1,0:T(2,128)S(1)} all-reduce(f32[2,16]{1,0:T(2,128)S(1)} %pad_maximum_fusion.9), channel_id=1, replica_groups=mesh['pole'=16,'slab'=32] {'slab'}, use_global_device_ids=true, to_apply=%region_11.12 | all-reduce | flops 32 | bytes 256 | tf_op jit(solution)/shard_map/psum | solution.py:109
  378.7 2.5 multiply_subtract_fusion.6
  383.1 80.1 %all-gather.5 = f32[32,2,16]{2,1,0:T(2,128)S(1)} all-gather(f32[1,2,16]{2,1,0:T(2,128)S(1)} %maximum_bitcast_fusion.2), channel_id=4, replica_groups=mesh['pole'=16,'slab'=32] {'slab'}, dimensions={0}, use_global_device_ids=true | all-gather | bytes 4224 | tf_op jit(solution)/shard_map/all_gather | solution.py:11
  466.1 1.9 collective-permute-start.4
  468.0 5.0 collective-permute-start.5
  473.2 4.8 collective-permute-done.4
  478.1 5.2 collective-permute-done.5
  484.9 76.8 %psum.51 = f32[2,16]{1,0:T(2,128)S(1)} all-reduce(f32[2,16]{1,0:T(2,128)S(1)} %pad_maximum_fusion.10), channel_id=1, replica_groups=mesh['pole'=16,'slab'=32] {'slab'}, use_global_device_ids=true, to_apply=%region_17.18 | all-reduce | flops 32 | bytes 256 | tf_op jit(solution)/shard_map/psum | solution.py:109
  561.8 1.6 multiply_subtract_fusion.1
  566.2 1.8 pad_maximum_fusion.6
  569.2 134.8 %all-reduce.4.cloned.1.call-done = (f32[2,16,4,16,128]{4,1,3,2,0:T(8,128)}, f32[2,16,4,16,128]{4,1,3,2,0:T(8,128)}) async-done(((f32[2,16,4,16,128]{4,1,3,2,0:T(8,128)}, f32[2,16,4,16,128]{4,1,3,2,0:T(8,128)}), (f32[2,16,4,16,128]{4,1,3,2,0:T(8,128)}, f32[2,16,4,16,128]{4,1,3,2,0:T(8,128)})) %all-reduce.4.cloned.1.call-update) | async-done | bytes 2097168 | tf_op jit(solution)/shard_map/psum | solution.py:121
  704.0 2.1 convolution_bitcast_fusion
  706.0 1.8 convolution_bitcast_fusion.2
  713.5 156.6 %all-reduce = (f32[2,16,16]{2,1,0:T(8,128)}, f32[2,16,16]{2,1,0:T(8,128)}) all-reduce(f32[2,16,16]{2,1,0:T(8,128)S(1)} %maximum_multiply_fusion, f32[2,16,16]{2,1,0:T(8,128)S(1)} %maximum_multiply_fusion.1), channel_id=1, replica_groups=mesh['pole'=16,'slab'=32] {'slab'}, use_global_device_ids=true, to_apply=%region_19.20 | all-reduce | flops 1024 | bytes 8192 | tf_op jit(solution)/shard_map/psum | solution.py:123
  (90 shorter events, 21.4 us)
Async XLA Ops:
  7.2 696.8 %all-reduce.4.cloned.1.call-start = ((), (), s32[]{:S(2)}) async-start(), calls=%async_computation | async-start | bytes 4194304 | tf_op jit(solution)/shard_map/psum | solution.py:121
  9.1 19.7 %collective-permute-start = (f32[2,16,1,16,128]{4,1,3,2,0:T(8,128)S(1)}, f32[2,16,1,16,128]{4,1,3,2,0:T(8,128)S(1)}, u32[]{:S(2)}, u32[]{:S(2)}) collective-permute-start(f32[2,16,1,16,128]{4,1,3,2,0:T(8,128)S(1)} %get-tuple-element.78), channel_id=1, source_target_pairs={{1,0},{2,1},{3,2},{4,3},{5,4},{6,5},{7,6},{8,7},{9,8},{10,9},{11,1... | collective-permute-start | bytes 786440 | tf_op jit(solution)/shard_map/ppermute | solution.py:23
  19.9 19.5 %collective-permute-start.1 = (f32[2,16,1,16,128]{4,1,3,2,0:T(8,128)S(1)}, f32[2,16,1,16,128]{4,1,3,2,0:T(8,128)S(1)}, u32[]{:S(2)}, u32[]{:S(2)}) collective-permute-start(f32[2,16,1,16,128]{4,1,3,2,0:T(8,128)S(1)} %get-tuple-element.79), channel_id=1, source_target_pairs={{0,1},{1,2},{2,3},{3,4},{4,5},{5,6},{6,7},{7,8},{8,9},{9,10},{10,1... | collective-permute-start | bytes 786440 | tf_op jit(solution)/shard_map/ppermute | solution.py:20
  24.9 1.8 copy-start.15
  200.0 1.2 copy-start
  282.6 12.5 %collective-permute-start.2 = (f32[2,16,1,16,128]{4,1,3,2,0:T(8,128)S(1)}, f32[2,16,1,16,128]{4,1,3,2,0:T(8,128)S(1)}, u32[]{:S(2)}, u32[]{:S(2)}) collective-permute-start(f32[2,16,1,16,128]{4,1,3,2,0:T(8,128)S(1)} %get-tuple-element.68), channel_id=1, source_target_pairs={{1,0},{2,1},{3,2},{4,3},{5,4},{6,5},{7,6},{8,7},{9,8},{10,9},{11,1... | collective-permute-start | bytes 786440 | tf_op jit(solution)/shard_map/ppermute | solution.py:23
  284.5 15.7 %collective-permute-start.3 = (f32[2,16,1,16,128]{4,1,3,2,0:T(8,128)S(1)}, f32[2,16,1,16,128]{4,1,3,2,0:T(8,128)S(1)}, u32[]{:S(2)}, u32[]{:S(2)}) collective-permute-start(f32[2,16,1,16,128]{4,1,3,2,0:T(8,128)S(1)} %get-tuple-element.69), channel_id=1, source_target_pairs={{0,1},{1,2},{2,3},{3,4},{4,5},{5,6},{6,7},{7,8},{8,9},{9,10},{10,1... | collective-permute-start | bytes 786440 | tf_op jit(solution)/shard_map/ppermute | solution.py:20
  300.9 1.0 copy-start.3
  381.3 0.8 copy-start.7
  381.4 1.4 copy-start.4
  463.3 1.0 copy-start.5
  463.3 1.2 copy-start.8
  466.1 12.0 %collective-permute-start.4 = (f32[2,16,1,16,128]{4,1,3,2,0:T(8,128)S(1)}, f32[2,16,1,16,128]{4,1,3,2,0:T(8,128)S(1)}, u32[]{:S(2)}, u32[]{:S(2)}) collective-permute-start(f32[2,16,1,16,128]{4,1,3,2,0:T(8,128)S(1)} %get-tuple-element.58), channel_id=1, source_target_pairs={{1,0},{2,1},{3,2},{4,3},{5,4},{6,5},{7,6},{8,7},{9,8},{10,9},{11,1... | collective-permute-start | bytes 786440 | tf_op jit(solution)/shard_map/ppermute | solution.py:23
  468.0 15.2 %collective-permute-start.5 = (f32[2,16,1,16,128]{4,1,3,2,0:T(8,128)S(1)}, f32[2,16,1,16,128]{4,1,3,2,0:T(8,128)S(1)}, u32[]{:S(2)}, u32[]{:S(2)}) collective-permute-start(f32[2,16,1,16,128]{4,1,3,2,0:T(8,128)S(1)} %get-tuple-element.59), channel_id=1, source_target_pairs={{0,1},{1,2},{2,3},{3,4},{4,5},{5,6},{6,7},{7,8},{8,9},{9,10},{10,1... | collective-permute-start | bytes 786440 | tf_op jit(solution)/shard_map/ppermute | solution.py:20
  484.0 1.0 copy-start.2
  561.8 1.8 copy-start.14
  563.4 1.0 copy-start.11
  563.4 1.2 copy-start.12
  563.4 1.3 copy-start.13
  565.0 1.0 copy-start.6
  565.0 1.2 copy-start.9
  704.0 2.1 copy-start.1
  707.8 1.6 copy-start.10
Sparse Core Ops, SparseCore 0:
  569.3 134.5 all-reduce.3
